TPU v7x, 256 devices: a whole 4x4x8 slice. The times are simulated.
256 devices in a mesh: tm: 64 (over y, x, z_hi), row: 4 (over z_lo, core).
Axes of the slice: x: 4, y: 4, z: 8 (z_hi: 4, z_lo: 2; z = z_hi * 2 + z_lo), core: 2. Of those that a mesh axis runs over, the one named last changes fastest.
Arguments:
- latent: bfloat16 [128, 8, 40, 2240], P('tm', 'row'), may hold values from -6 to 6
- query_raw: bfloat16 [128, 8, 40, 2240], P('tm', 'row'), may hold values from -6 to 6
- key_raw: bfloat16 [128, 8, 40, 2240], P('tm', 'row'), may hold values from -12 to 12
- value_raw: bfloat16 [128, 8, 40, 2240], P('tm', 'row'), may hold values from -12 to 12
- query_gain: float32 [2240], replicated, may hold values from 0.4 to 2.5
- key_gain: float32 [2240], replicated, may hold values from 0.4 to 2.5
- space_kernel: float32 [3, 3, 2240], replicated, may hold values from -2 to 2
- time_kernel: float32 [3, 2240], replicated, may hold values from -3.5 to 3.5
- first_weight: bfloat16 [2240, 2048], P('tm', 'row'), may hold values from -0.125 to 0.125
- first_bias: float32 [2048], replicated, may hold values from -3 to 3
- second_weight: bfloat16 [2048, 1280], P('row', 'tm'), may hold values from -0.125 to 0.125
- second_bias: float32 [1280], replicated, may hold values from -3 to 3
- target_keys: bfloat16 [128, 256, 1280], P('tm', 'row'), may hold values from -410 to 410
- target_values: bfloat16 [128, 256, 1280], P('tm', 'row'), may hold values from -12 to 12
Outputs:
- blended: bfloat16 [128, 8, 40, 2240], P('tm', 'row')
- attended: bfloat16 [128, 8, 40, 1280], P('tm', 'row')
All inputs are finite; a program needn't handle non-finite values.
Results may differ from a plain program's by a relative error of at most 0.01545.
The roundings to bfloat16 on the way count: a program that leaves them out, or rounds other values in their place, can miss the bound.
Values may be sent and summed in bfloat16 or wider, within the bound.
No kernel may reach another device: no remote copies, remote signals or barrier semaphores. Data moves between devices by JAX's collectives and lax.ppermute only.
A program may use at most 128 MiB of HBM per device.

v0:
```python
import jax
import jax.numpy as jnp
from jax import lax
from jax.sharding import PartitionSpec as P

HEADS = 70
HEAD_DIM = 32
AHEADS = 16
AHEAD_DIM = 80


def prefix(value, axis, combine, identity):
    length, index = (lax.axis_size(axis), lax.axis_index(axis))
    everything = jax.tree.map(lambda part: lax.all_gather(part, axis), value)
    start = jax.tree.map(
        lambda part, zero: jnp.broadcast_to(jnp.asarray(zero, part.dtype), part.shape),
        value,
        identity,
    )

    def lap(k, before):
        reached = k < index
        new = combine(before, jax.tree.map(lambda part: part[k], everything))
        return jax.tree.map(lambda a, b: jnp.where(reached, a, b), new, before)

    return lax.fori_loop(0, length, lap, start)


def extended(block, sides, width):
    for axis, dim in sides:
        count = lax.axis_size(axis)
        forward = [(i, i + 1) for i in range(count - 1)]
        backward = [(target, source) for source, target in forward]
        low = lax.ppermute(
            lax.slice_in_dim(block, block.shape[dim] - width, None, axis=dim), axis, forward
        )
        high = lax.ppermute(lax.slice_in_dim(block, 0, width, axis=dim), axis, backward)
        block = jnp.concatenate([low, block, high], axis=dim)
    return block


def head_features(source, scaling):
    values = source.astype(jnp.float32).reshape(source.shape[:-1] + (HEADS, HEAD_DIM))
    mean_square = jnp.maximum(jnp.mean(values * values, axis=-1, keepdims=True), 0.25)
    return jax.nn.relu(values * lax.rsqrt(mean_square) * scaling.reshape(HEADS, HEAD_DIM))


def add_pair(earlier, later):
    return (earlier[0] + later[0], earlier[1] + later[1])


def contraction(left, piece):
    return jnp.dot(left, piece, preferred_element_type=jnp.float32)


def softmax_fold(query_split, frames_here, running, pieces):
    score_scale = 1.0 / AHEAD_DIM**0.5
    best, totals, gathered = running
    key_part, value_part = pieces
    piece_rows = key_part.shape[1]
    key_split = key_part.reshape(frames_here, piece_rows, AHEADS, AHEAD_DIM)
    value_split = value_part.reshape(frames_here, piece_rows, AHEADS, AHEAD_DIM)
    scores = (
        jnp.einsum("cqgd,ckgd->cgkq", query_split, key_split, preferred_element_type=jnp.float32)
        * score_scale
    )
    newest = jnp.max(scores, axis=2)
    fading = jnp.exp(best - newest)
    weights = jnp.exp(scores - newest[:, :, None, :])
    totals = totals * fading + jnp.sum(weights, axis=2)
    update = jnp.einsum(
        "cgkq,ckgd->cqgd",
        weights.astype(jnp.bfloat16),
        value_split,
        preferred_element_type=jnp.float32,
    )
    gathered = gathered * jnp.transpose(fading, (0, 2, 1))[..., None] + update
    return (newest, totals, gathered)


def per_device(
    latent,
    query_raw,
    key_raw,
    value_raw,
    query_gain,
    key_gain,
    space_kernel,
    time_kernel,
    first_weight,
    first_bias,
    second_weight,
    second_bias,
    target_keys,
    target_values,
):
    frames_here, rows_here, cols_here, model_width = latent.shape
    token_count = frames_here * rows_here * cols_here
    query_feat = head_features(query_raw, query_gain)
    key_feat = head_features(key_raw, key_gain)
    value_feat = value_raw.astype(jnp.float32).reshape(key_feat.shape)
    local_state = jnp.einsum(
        "crwhd,crwhe->dhe", key_feat, value_feat, precision=lax.Precision.HIGHEST
    ).reshape(HEAD_DIM, model_width)
    local_keys = jnp.sum(key_feat, axis=(0, 1, 2)).reshape(model_width)
    block_state, block_keys = lax.psum((local_state, local_keys), "row")
    earlier_state, earlier_keys = prefix(
        (block_state, block_keys),
        "tm",
        add_pair,
        (jnp.zeros_like(block_state), jnp.zeros_like(block_keys)),
    )
    key_state = (earlier_state + block_state).reshape(HEAD_DIM, HEADS, HEAD_DIM)
    key_total = (earlier_keys + block_keys).reshape(HEADS, HEAD_DIM)
    numerator = jnp.einsum(
        "crwhd,dhe->crwhe", query_feat, key_state, precision=lax.Precision.HIGHEST
    )
    denominator = (
        jnp.einsum("crwhd,hd->crwh", query_feat, key_total, precision=lax.Precision.HIGHEST) + 1e-06
    )
    linear_out = (numerator / denominator[..., None]).reshape(latent.shape)
    hidden_in = (latent.astype(jnp.float32) + linear_out).astype(jnp.bfloat16)
    time_padded = extended(hidden_in, (("tm", 0),), 1)
    row_padded = extended(hidden_in, (("row", 1),), 1)
    row_padded = jnp.pad(row_padded, ((0, 0), (0, 0), (1, 1), (0, 0)))
    center = hidden_in.astype(jnp.float32)
    spatial = jnp.zeros(center.shape, jnp.float32)
    for shift_row in range(3):
        for shift_col in range(3):
            spatial = spatial + space_kernel[shift_row, shift_col] * row_padded[
                :, shift_row : shift_row + rows_here, shift_col : shift_col + cols_here
            ].astype(jnp.float32)
    temporal = jnp.zeros(center.shape, jnp.float32)
    for shift_time in range(3):
        temporal = temporal + time_kernel[shift_time] * time_padded[
            shift_time : shift_time + frames_here
        ].astype(jnp.float32)
    blended = (center + spatial + temporal).astype(jnp.bfloat16)
    tokens = blended.reshape(token_count, model_width)
    first_full = lax.all_gather(first_weight, "row", axis=1, tiled=True)
    linear_part = contraction(tokens, lax.all_gather(first_full, "tm", axis=0, tiled=True))
    hidden_units = jax.nn.silu(linear_part + first_bias).astype(jnp.bfloat16)
    second_full = lax.all_gather(second_weight, "row", axis=0, tiled=True)
    queries = (
        jnp.dot(
            hidden_units,
            lax.all_gather(second_full, "tm", axis=1, tiled=True),
            preferred_element_type=jnp.float32,
        )
        + second_bias
    ).astype(jnp.bfloat16)
    frame_tokens = rows_here * cols_here
    feature_count = queries.shape[1]
    query_split = queries.reshape(frames_here, frame_tokens, AHEADS, AHEAD_DIM)
    starting = (
        jnp.full((frames_here, AHEADS, frame_tokens), -jnp.inf, jnp.float32),
        jnp.zeros((frames_here, AHEADS, frame_tokens), jnp.float32),
        jnp.zeros((frames_here, frame_tokens, AHEADS, AHEAD_DIM), jnp.float32),
    )
    best, totals, gathered = softmax_fold(
        query_split,
        frames_here,
        starting,
        (
            lax.all_gather(target_keys, "row", axis=1, tiled=True),
            lax.all_gather(target_values, "row", axis=1, tiled=True),
        ),
    )
    attended = (gathered / jnp.transpose(totals, (0, 2, 1))[..., None]).astype(jnp.bfloat16)
    attended = attended.reshape(frames_here, rows_here, cols_here, feature_count)
    return (blended, attended)


def solution(mesh):
    return jax.shard_map(
        per_device,
        mesh=mesh,
        in_specs=(
            P("tm", "row", None, None),
            P("tm", "row", None, None),
            P("tm", "row", None, None),
            P("tm", "row", None, None),
            P(),
            P(),
            P(),
            P(),
            P("tm", "row"),
            P(),
            P("row", "tm"),
            P(),
            P("tm", "row", None),
            P("tm", "row", None),
        ),
        out_specs=(P("tm", "row", None, None), P("tm", "row", None, None)),
        check_vma=False,
    )
```

profile of v0, /device:TPU:1, one launch (start us, length us, event | category | flops | bytes accessed | tf_op | source)
XLA Modules:
  0.0 1391.0 jit_solution(9008204149038718238)
XLA Ops:
  7.2 4.9 reshape.85
  12.2 5.5 multiply_reduce_fusion.1
  25.7 4.8 fusion.24
  41.7 11.7 psum.15
  56.0 7.9 all_gather.36
  64.0 6.0 all_gather.34
  70.0 7.9 all-reduce.5.cloned.1.call-done
  81.8 5.6 multiply_reduce_fusion
  91.2 6.1 copy.38
  98.7 640.2 %all-reduce.7.cloned.1.call-done = f32[143360]{0:T(1024)} async-done(((f32[143360]{0:T(1024)}), f32[143360]{0:T(1024)}) %all-reduce.7.cloned.1.call-update) | async-done | bytes 573456
  740.2 51.9 %all-gather.10.cloned.1.call-done = bf16[2,256,1280]{2,1,0:T(8,128)(2,1)} async-done(((bf16[2,64,1280]{2,1,0:T(8,128)(2,1)}), bf16[2,256,1280]{2,1,0:T(8,128)(2,1)}) %all-gather.10.cloned.1.call-update) | async-done | bytes 1310736 | tf_op jit(solution)/shard_map/all_gather | solution.py:165
  793.7 25.8 %all-gather.12.cloned.1.call-done = bf16[2,256,1280]{2,1,0:T(8,128)(2,1)} async-done(((bf16[2,64,1280]{2,1,0:T(8,128)(2,1)}), bf16[2,256,1280]{2,1,0:T(8,128)(2,1)}) %all-gather.12.cloned.1.call-update) | async-done | bytes 1310736 | tf_op jit(solution)/shard_map/all_gather | solution.py:166
  821.9 99.5 %all-gather.18.cloned.1.call-done = bf16[64,20,2048]{2,1,0:T(8,128)(2,1)} async-done(((bf16[1,20,2048]{2,1,0:T(8,128)(2,1)}), bf16[64,20,2048]{2,1,0:T(8,128)(2,1)}) %all-gather.18.cloned.1.call-update) | async-done | bytes 5242896 | tf_op jit(solution)/shard_map/all_gather | solution.py:147
  921.4 9.0 reshape.108
  930.4 122.6 %all-gather.16.cloned.1.call-done = bf16[64,35,2048]{2,1,0:T(8,128)(2,1)} async-done(((bf16[1,35,2048]{2,1,0:T(8,128)(2,1)}), bf16[64,35,2048]{2,1,0:T(8,128)(2,1)}) %all-gather.16.cloned.1.call-update) | async-done | bytes 9175056 | tf_op jit(solution)/shard_map/all_gather | solution.py:141
  1053.0 10.7 reshape.106
  1063.7 162.4 %all-gather.14.cloned.1.call-done = f32[2048,2240]{1,0:T(8,128)} async-done(((f32[32,2240]{1,0:T(8,128)}), f32[2048,2240]{1,0:T(8,128)}) %all-gather.14.cloned.1.call-update) | async-done | bytes 18350096 | tf_op jit(solution)/shard_map/all_gather | solution.py:14
  1226.1 72.9 %while.16 = (s32[]{:T(128)}, f32[32,2240]{1,0:T(8,128)S(1)}, f32[2240]{0:T(1024)S(1)}, s32[]{:T(128)}, f32[64,32,2240]{2,1,0:T(8,128)}, /*index=5*/f32[64,2240]{1,0:T(8,128)S(1)}, s32[]{:T(128)}, s32[]{:T(128)}) while((s32[]{:T(128)}, f32[32,2240]{1,0:T(8,128)S(1)}, f32[2240]{0:T(1024)S(1)}, s32[]{:T(128)}, ...), condition=%wide.region_5.6_spmd.clone, body=%wide.region_4.5_spmd.clone.sunk | while | flops 221764 | bytes 905075 | solution.py:26
  1305.3 8.9 bitcast_divide_fusion
  1314.2 6.1 copy.39
  1324.6 15.7 %collective-permute-start = (bf16[2,1,40,2240]{3,2,1,0:T(8,128)(2,1)S(1)}, bf16[2,1,40,2240]{3,2,1,0:T(8,128)(2,1)S(1)}, u32[]{:S(2)}, u32[]{:S(2)}) collective-permute-start(bf16[2,1,40,2240]{3,2,1,0:T(8,128)(2,1)S(1)} %get-tuple-element.159), channel_id=1, source_target_pairs={{0,1},{1,2},{2,3},{4,5},{5,6},{6,7},{8,9},{9,10},{10,11},{12,13},{... | collective-permute-start | bytes 1075208 | tf_op jit(solution)/shard_map/ppermute | solution.py:34
  1349.6 5.2 collective-permute-done.2
  1354.9 11.4 collective-permute-done.3
  1368.8 8.8 fusion.5
  (308 shorter events, 134.1 us)
Async XLA Ops:
  7.2 70.7 %all-reduce.5.cloned.1.call-start = ((), (), s32[]{:S(2)}) async-start(), calls=%async_computation | async-start | bytes 589824 | tf_op jit(solution)/shard_map/psum | solution.py:106
  32.2 706.7 %all-reduce.7.cloned.1.call-start = ((), (), s32[]{:S(2)}) async-start(), calls=%async_computation.4 | async-start | bytes 1146880
  41.4 14.6 %copy-start.21 = (bf16[512,20]{0,1:T(8,128)(2,1)S(1)}, bf16[512,20]{0,1:T(8,128)(2,1)}, u32[]{:S(2)}) copy-start(bf16[512,20]{0,1:T(8,128)(2,1)} %param.26) | copy-start | bytes 61444
  41.4 22.6 %copy-start.20 = (bf16[35,512]{1,0:T(8,128)(2,1)S(1)}, bf16[35,512]{1,0:T(8,128)(2,1)}, u32[]{:S(2)}) copy-start(bf16[35,512]{1,0:T(8,128)(2,1)} %param.24) | copy-start | bytes 107524
  41.7 36.3 %copy-start.5 = (bf16[2,2,40,2240]{3,2,1,0:T(8,128)(2,1)S(1)}, bf16[2,2,40,2240]{3,2,1,0:T(8,128)(2,1)}, u32[]{:S(2)}) copy-start(bf16[2,2,40,2240]{3,2,1,0:T(8,128)(2,1)} %param.17) | copy-start | bytes 2150404
  54.6 737.5 %all-gather.10.cloned.1.call-start = ((), (), s32[]{:S(2)}) async-start(), calls=%async_computation.1 | async-start | bytes 1638400 | tf_op jit(solution)/shard_map/all_gather | solution.py:165
  55.3 764.1 %all-gather.12.cloned.1.call-start = ((), (), s32[]{:S(2)}) async-start(), calls=%async_computation.2 | async-start | bytes 1638400 | tf_op jit(solution)/shard_map/all_gather | solution.py:166
  55.9 865.4 %all-gather.18.cloned.1.call-start = ((), (), s32[]{:S(2)}) async-start(), calls=%async_computation.6 | async-start | bytes 6389760 | tf_op jit(solution)/shard_map/all_gather | solution.py:147
  63.9 989.0 %all-gather.16.cloned.1.call-start = ((), (), s32[]{:S(2)}) async-start(), calls=%async_computation.5 | async-start | bytes 10649600 | tf_op jit(solution)/shard_map/all_gather | solution.py:141
  70.0 1156.1 %all-gather.14.cloned.1.call-start = ((), (), s32[]{:S(2)}) async-start(), calls=%async_computation.3 | async-start | bytes 19169280 | tf_op jit(solution)/shard_map/all_gather | solution.py:14
  1324.6 22.5 %collective-permute-start = (bf16[2,1,40,2240]{3,2,1,0:T(8,128)(2,1)S(1)}, bf16[2,1,40,2240]{3,2,1,0:T(8,128)(2,1)S(1)}, u32[]{:S(2)}, u32[]{:S(2)}) collective-permute-start(bf16[2,1,40,2240]{3,2,1,0:T(8,128)(2,1)S(1)} %get-tuple-element.159), channel_id=1, source_target_pairs={{0,1},{1,2},{2,3},{4,5},{5,6},{6,7},{8,9},{9,10},{10,11},{12,13},{... | collective-permute-start | bytes 1075208 | tf_op jit(solution)/shard_map/ppermute | solution.py:34
  1340.3 8.8 collective-permute-start.1
  1342.3 24.0 %copy-start.9 = (f32[2240]{0:T(1024)S(1)}, f32[2240]{0:T(1024)}, u32[]{:S(2)}) copy-start(f32[2240]{0:T(1024)} %get-tuple-element.137) | copy-start | bytes 26884
  1342.3 24.0 %copy-start.10 = (f32[2240]{0:T(1024)S(1)}, f32[2240]{0:T(1024)}, u32[]{:S(2)}) copy-start(f32[2240]{0:T(1024)} %get-tuple-element.138) | copy-start | bytes 26884
  1342.3 24.0 %copy-start.11 = (f32[2240]{0:T(1024)S(1)}, f32[2240]{0:T(1024)}, u32[]{:S(2)}) copy-start(f32[2240]{0:T(1024)} %get-tuple-element.139) | copy-start | bytes 26884
  1342.3 23.9 %copy-start.12 = (f32[2240]{0:T(1024)S(1)}, f32[2240]{0:T(1024)}, u32[]{:S(2)}) copy-start(f32[2240]{0:T(1024)} %get-tuple-element.140) | copy-start | bytes 26884
  1342.3 23.9 %copy-start.13 = (f32[2240]{0:T(1024)S(1)}, f32[2240]{0:T(1024)}, u32[]{:S(2)}) copy-start(f32[2240]{0:T(1024)} %get-tuple-element.141) | copy-start | bytes 26884
  1342.3 23.9 %copy-start.14 = (f32[2240]{0:T(1024)S(1)}, f32[2240]{0:T(1024)}, u32[]{:S(2)}) copy-start(f32[2240]{0:T(1024)} %get-tuple-element.142) | copy-start | bytes 26884
  1342.3 23.9 %copy-start.15 = (f32[2240]{0:T(1024)S(1)}, f32[2240]{0:T(1024)}, u32[]{:S(2)}) copy-start(f32[2240]{0:T(1024)} %get-tuple-element.143) | copy-start | bytes 26884
  1342.3 23.9 %copy-start.17 = (f32[2240]{0:T(1024)S(1)}, f32[2240]{0:T(1024)}, u32[]{:S(2)}) copy-start(f32[2240]{0:T(1024)} %get-tuple-element.144) | copy-start | bytes 26884
  1342.4 23.9 %copy-start.18 = (f32[2240]{0:T(1024)S(1)}, f32[2240]{0:T(1024)}, u32[]{:S(2)}) copy-start(f32[2240]{0:T(1024)} %get-tuple-element.145) | copy-start | bytes 26884
  1342.4 23.9 %copy-start.19 = (f32[2240]{0:T(1024)S(1)}, f32[2240]{0:T(1024)}, u32[]{:S(2)}) copy-start(f32[2240]{0:T(1024)} %get-tuple-element.146) | copy-start | bytes 26884
  1342.4 12.5 collective-permute-start.2
  1345.9 20.4 %collective-permute-start.3 = (bf16[1,2,40,2240]{3,2,1,0:T(8,128)(2,1)S(1)}, bf16[1,2,40,2240]{3,2,1,0:T(8,128)(2,1)S(1)}, u32[]{:S(2)}, u32[]{:S(2)}) collective-permute-start(bf16[1,2,40,2240]{3,2,1,0:T(8,128)(2,1)S(1)} %get-tuple-element.162), channel_id=1, source_target_pairs={{4,0},{8,4},{12,8},{16,12},{20,16},{24,20},{28,24},{32,28},{36,32}... | collective-permute-start | bytes 1075208 | tf_op jit(solution)/shard_map/ppermute | solution.py:37
  (14 other events, 62.2 us)
Sparse Core Ops, SparseCore 0:
  32.3 45.5 all-reduce.4
  81.1 657.7 all-reduce.6
  740.7 51.2 all-gather.9
  793.7 25.6 all-gather.11
  822.6 98.7 all-gather.17
  924.5 128.4 all-gather.15
  1056.3 169.7 all-gather.13
where the time goes:
time: 1400 us; the launch traced here: 1390 us
  waiting for transfers between devices  1130 us (81%)
  other arithmetic  91.3 us (7%)
  local copies, waits for them, and re-layouts  73.7 us (5%)
  matrix products  29.4 us (2%)
  blocking collectives  25.6 us (2%)
  starting transfers between devices  22.6 us (2%)
  between operations  15.8 us (1%)
    unnamed x8, waiting for transfers between devices  641 us
    all_gather x1, waiting for transfers between devices, prefix(): everything = jax.tree.map(lambda part: lax.all_gather(part, axis), value)  162 us
    all_gather x1, waiting for transfers between devices, per_device(): lax.all_gather(first_full, 'tm', axis=0, tiled=True)  123 us
    all_gather x1, waiting for transfers between devices, per_device(): lax.all_gather(second_full, 'tm', axis=1, tiled=True)  99.5 us
    select_n x128, other arithmetic, lap(): return jax.tree.map(lambda a, b: jnp.where(reached, a, b), new, before)  67.8 us
    all_gather x1, waiting for transfers between devices, per_device(): lax.all_gather(target_keys, 'row', axis=1, tiled=True)  51.9 us
  transfers between devices with their start and end apart: 11, of which 10 were waited for; matrix products, arithmetic and copies ran while one was open for 4% of the time, Pallas kernels for 0%

commit v1 on v0

v1 whole, which is shorter than its diff:
```python
import jax
import jax.numpy as jnp
from jax import lax
from jax.experimental import pallas as pl
from jax.experimental.pallas import tpu as pltpu
from jax.sharding import PartitionSpec as P

HEADS = 70
HEAD_DIM = 32
AHEADS = 16
AHEAD_DIM = 80
D = 2240
GROUPS = 18
LANES = 384
STEPS = 6
PER_STEP = LANES // 128
TOKENS = 160
STATE_ROWS = 608
KEY_ROW = GROUPS * HEAD_DIM
LINE_K = 140
LINE_PAD = 144
PADDED = 16 * LINE_PAD
PROJ = 2048
OUTF = 1280
FRAME_TOKENS = 80
BOTH = ("tm", "row")
F32 = jnp.float32
BF16 = jnp.bfloat16


def block_ones():
    rows = lax.broadcasted_iota(jnp.int32, (128, 128), 0) // HEAD_DIM
    cols = lax.broadcasted_iota(jnp.int32, (128, 128), 1) // HEAD_DIM
    return rows == cols


def split(value):
    high = value.astype(BF16)
    return high, (value - high.astype(F32)).astype(BF16)


def dot(left, right, dims=((1,), (0,))):
    return lax.dot_general(left, right, (dims, ((), ())), preferred_element_type=F32)


def features(raw, gain, ones):
    square_high, square_low = split(raw * raw)
    mean = (dot(square_high, ones) + dot(square_low, ones)) * (1.0 / HEAD_DIM)
    return jnp.maximum(raw * lax.rsqrt(jnp.maximum(mean, 0.25)) * gain, 0.0)


def lane_mask(step, j, rows):
    lane = lax.broadcasted_iota(jnp.int32, (rows, 128), 1)
    return lane + (step * LANES + j * 128) < D


def state_kernel(key_ref, value_ref, gain_ref, out_ref):
    step = pl.program_id(0)

    @pl.when(step == 0)
    def _():
        out_ref[KEY_ROW:STATE_ROWS, :] = jnp.zeros((STATE_ROWS - KEY_ROW, 128), F32)

    same = block_ones()
    ones = jnp.where(same, 1.0, 0.0).astype(BF16)
    for j in range(PER_STEP):
        lanes = slice(j * 128, (j + 1) * 128)
        mask = lane_mask(step, j, TOKENS)
        raw = jnp.where(mask, key_ref[:, lanes].astype(F32), 0.0)
        value = jnp.where(mask, value_ref[:, lanes].astype(F32), 0.0).astype(BF16)
        gain = jnp.where(lane_mask(step, j, 1), gain_ref[:, lanes], 0.0)
        feat = features(raw, gain, ones)
        high, low = split(feat)
        product = dot(high, value, ((0,), (0,))) + dot(low, value, ((0,), (0,)))
        product = jnp.where(same, product, 0.0)
        compact = product[0:32] + product[32:64] + product[64:96] + product[96:128]
        group = step * PER_STEP + j
        out_ref[pl.ds(pl.multiple_of(group * HEAD_DIM, HEAD_DIM), HEAD_DIM), :] = compact
        out_ref[pl.ds(KEY_ROW + group, 1), :] = jnp.sum(feat, axis=0, keepdims=True)


def local_state(key_raw, value_raw, key_gain):
    return pl.pallas_call(
        state_kernel,
        grid=(STEPS,),
        in_specs=[
            pl.BlockSpec((TOKENS, LANES), lambda i: (0, i)),
            pl.BlockSpec((TOKENS, LANES), lambda i: (0, i)),
            pl.BlockSpec((1, LANES), lambda i: (0, i)),
        ],
        out_specs=pl.BlockSpec((STATE_ROWS, 128), lambda i: (0, 0)),
        out_shape=jax.ShapeDtypeStruct((STATE_ROWS, 128), F32),
        name="local_state",
    )(key_raw, value_raw, key_gain)


def apply_kernel(query_ref, latent_ref, gain_ref, state_ref, out_ref):
    step = pl.program_id(0)
    same = block_ones()
    ones = jnp.where(same, 1.0, 0.0).astype(BF16)
    for j in range(PER_STEP):
        lanes = slice(j * 128, (j + 1) * 128)
        raw = jnp.where(lane_mask(step, j, TOKENS), query_ref[:, lanes].astype(F32), 0.0)
        gain = jnp.where(lane_mask(step, j, 1), gain_ref[:, lanes], 0.0)
        feat = features(raw, gain, ones)
        group = step * PER_STEP + j
        compact = state_ref[pl.ds(pl.multiple_of(group * HEAD_DIM, HEAD_DIM), HEAD_DIM), :]
        keys = state_ref[pl.ds(KEY_ROW + group, 1), :]
        wide = jnp.where(same, jnp.concatenate([compact] * 4, axis=0), 0.0)
        wide_high, wide_low = split(wide)
        high, low = split(feat)
        numerator = dot(high, wide_high) + dot(low, wide_high) + dot(high, wide_low)
        scaled_high, scaled_low = split(feat * keys)
        denominator = dot(scaled_high, ones) + dot(scaled_low, ones) + 1e-06
        out_ref[:, lanes] = (latent_ref[:, lanes].astype(F32) + numerator / denominator).astype(
            BF16
        )


def apply_state(query_raw, latent, query_gain, state):
    return pl.pallas_call(
        apply_kernel,
        grid=(STEPS,),
        in_specs=[
            pl.BlockSpec((TOKENS, LANES), lambda i: (0, i)),
            pl.BlockSpec((TOKENS, LANES), lambda i: (0, i)),
            pl.BlockSpec((1, LANES), lambda i: (0, i)),
            pl.BlockSpec((STATE_ROWS, 128), lambda i: (0, 0)),
        ],
        out_specs=pl.BlockSpec((TOKENS, LANES), lambda i: (0, i)),
        out_shape=jax.ShapeDtypeStruct((TOKENS, D), BF16),
        name="apply_state",
    )(query_raw, latent, query_gain, state)


def mix_kernel(
    own_ref, before_ref, after_ref, above_ref, below_ref, space_ref, time_ref, out_ref, pad_ref, last_ref
):
    step = pl.program_id(0)
    column = lax.broadcasted_iota(jnp.int32, (40, 128), 0)
    for j in range(PER_STEP):
        lanes = slice(j * 128, (j + 1) * 128)
        space = [[space_ref[3 * a + b : 3 * a + b + 1, lanes] for b in range(3)] for a in range(3)]
        time = [time_ref[a : a + 1, lanes] for a in range(3)]
        middle = 1.0 + space[1][1] + time[1]
        own = [[own_ref[f, r, :, lanes].astype(F32) for r in range(2)] for f in range(2)]
        before = [before_ref[r, :, lanes].astype(F32) for r in range(2)]
        after = [after_ref[r, :, lanes].astype(F32) for r in range(2)]
        above = [above_ref[f, :, lanes].astype(F32) for f in range(2)]
        below = [below_ref[f, :, lanes].astype(F32) for f in range(2)]
        tiles = []
        for f in range(2):
            for r in range(2):
                up = above[f] if r == 0 else own[f][0]
                down = below[f] if r == 1 else own[f][1]
                here = own[f][r]
                past = before[r] if f == 0 else own[0][r]
                future = after[r] if f == 1 else own[1][r]
                left = space[0][0] * up + space[1][0] * here + space[2][0] * down
                right = space[0][2] * up + space[1][2] * here + space[2][2] * down
                total = middle * here + space[0][1] * up + space[2][1] * down
                total = total + time[0] * past + time[2] * future
                total = total + jnp.where(column == 0, 0.0, pltpu.roll(left, 1, 0))
                total = total + jnp.where(column == 39, 0.0, pltpu.roll(right, 39, 0))
                tile = total.astype(BF16)
                out_ref[f, r, :, lanes] = tile
                tiles.append(total)
        whole = jnp.concatenate(tiles, axis=0)
        whole = jnp.where(lane_mask(step, j, TOKENS), whole, 0.0).astype(BF16)
        previous = last_ref[...]
        if j == 0:
            previous = jnp.where(step == 0, jnp.zeros_like(previous), previous)
        start = step * LANES + j * 128
        target = lax.broadcasted_iota(jnp.int32, (128, 128), 1) + start
        line = (target * 3641) >> 19
        inside = target - line * LINE_PAD
        source = line * LINE_K + inside - start
        row = lax.broadcasted_iota(jnp.int32, (128, 128), 0)
        valid = inside < LINE_K
        here_pick = jnp.where((source == row) & valid, 1.0, 0.0).astype(BF16)
        past_pick = jnp.where((source + 128 == row) & valid, 1.0, 0.0).astype(BF16)
        pad_ref[:, lanes] = (dot(whole, here_pick) + dot(previous, past_pick)).astype(BF16)
        last_ref[...] = whole


def mix(own, before, after, above, below, space_kernel, time_kernel):
    halo = pl.BlockSpec((2, 40, LANES), lambda i: (0, 0, i))
    return pl.pallas_call(
        mix_kernel,
        grid=(STEPS,),
        in_specs=[
            pl.BlockSpec((2, 2, 40, LANES), lambda i: (0, 0, 0, i)),
            halo,
            halo,
            halo,
            halo,
            pl.BlockSpec((9, LANES), lambda i: (0, i)),
            pl.BlockSpec((3, LANES), lambda i: (0, i)),
        ],
        out_specs=[
            pl.BlockSpec((2, 2, 40, LANES), lambda i: (0, 0, 0, i)),
            pl.BlockSpec((TOKENS, LANES), lambda i: (0, i)),
        ],
        out_shape=[
            jax.ShapeDtypeStruct((2, 2, 40, D), BF16),
            jax.ShapeDtypeStruct((TOKENS, PADDED), BF16),
        ],
        scratch_shapes=[pltpu.VMEM((TOKENS, 128), BF16)],
        name="mix",
    )(own, before, after, above, below, space_kernel, time_kernel)


CHUNK = 512
CHUNKS = PROJ // CHUNK


def project_kernel(
    token_ref,
    first_bias_ref,
    second_bias_ref,
    key_ref,
    value_ref,
    weight_ref,
    out_ref,
    first_ref,
    second_ref,
    hidden_ref,
    query_ref,
    first_sem,
    second_sem,
):
    def first_copy(n):
        return pltpu.make_async_copy(
            weight_ref.at[:, pl.ds(0, LINE_PAD), pl.ds(n * CHUNK, CHUNK)],
            first_ref.at[n],
            first_sem.at[n],
        )

    second_copy = pltpu.make_async_copy(
        weight_ref.at[:, pl.ds(LINE_PAD, AHEAD_DIM), :], second_ref, second_sem
    )
    for n in range(CHUNKS):
        first_copy(n).start()
    second_copy.start()
    for n in range(CHUNKS):
        first_copy(n).wait()
        columns = slice(n * CHUNK, (n + 1) * CHUNK)
        part = dot(token_ref[...], first_ref[n].reshape(PADDED, CHUNK)) + first_bias_ref[:, columns]
        hidden_ref[:, columns] = (part * jax.nn.sigmoid(part)).astype(BF16)
    second_copy.wait()
    query_ref[...] = (
        dot(hidden_ref[...], second_ref[...].reshape(OUTF, PROJ), ((1,), (1,))) + second_bias_ref[...]
    ).astype(BF16)
    scale = 1.0 / AHEAD_DIM**0.5
    lane = lax.broadcasted_iota(jnp.int32, (FRAME_TOKENS, 256), 1)
    for f in range(2):
        rows = slice(f * FRAME_TOKENS, (f + 1) * FRAME_TOKENS)
        tiles = [jnp.zeros((FRAME_TOKENS, 128), F32) for _ in range(OUTF // 128)]
        for head in range(AHEADS):
            tile = min(head * AHEAD_DIM // 128, OUTF // 128 - 2)
            begin = head * AHEAD_DIM - tile * 128
            window = slice(tile * 128, tile * 128 + 256)
            mine = (lane >= begin) & (lane < begin + AHEAD_DIM)
            query = query_ref[rows, window]
            query = jnp.where(mine, query, jnp.zeros_like(query))
            scores = dot(query, key_ref[f, :, window], ((1,), (1,))) * scale
            weights = jnp.exp(scores - jnp.max(scores, axis=1, keepdims=True))
            totals = jnp.sum(weights, axis=1, keepdims=True)
            result = dot(weights.astype(BF16), value_ref[f, :, window]) / totals
            result = jnp.where(mine, result, 0.0)
            tiles[tile] = tiles[tile] + result[:, :128]
            tiles[tile + 1] = tiles[tile + 1] + result[:, 128:]
        for index, tile in enumerate(tiles):
            out_ref[rows, index * 128 : (index + 1) * 128] = tile.astype(BF16)


def project_attend(tokens, first_bias, second_bias, keys, values, weights):
    vmem = pl.BlockSpec(memory_space=pltpu.VMEM)
    return pl.pallas_call(
        project_kernel,
        in_specs=[vmem] * 5 + [pl.BlockSpec(memory_space=pl.ANY)],
        out_specs=vmem,
        out_shape=jax.ShapeDtypeStruct((TOKENS, OUTF), BF16),
        scratch_shapes=[
            pltpu.VMEM((CHUNKS, 16, LINE_PAD, CHUNK), BF16),
            pltpu.VMEM((16, AHEAD_DIM, PROJ), BF16),
            pltpu.VMEM((TOKENS, PROJ), BF16),
            pltpu.VMEM((TOKENS, OUTF), BF16),
            pltpu.SemaphoreType.DMA((CHUNKS,)),
            pltpu.SemaphoreType.DMA,
        ],
        name="project_attend",
    )(tokens, first_bias, second_bias, keys, values, weights)


def line_groups():
    return [[line * 16 + i for i in range(16)] for line in range(16)]


def plane_groups():
    return [[line * 16 + i for line in range(16)] for i in range(16)]


def shifted(value, stride, distance):
    pairs = []
    for t in range(64):
        digit = (t // stride) % 4
        pairs.append((t, t + ((digit + distance) % 4 - digit) * stride))
    return lax.ppermute(value, "tm", pairs)


def ring_prefix(value, stride):
    digit = (lax.axis_index("tm") // stride) % 4
    moved = [shifted(value, stride, distance) for distance in (1, 2, 3)]
    earlier = sum(jnp.where(digit >= d + 1, part, 0.0) for d, part in enumerate(moved))
    return earlier, value + moved[0] + moved[1] + moved[2]


def state_prefix(local):
    pieces = lax.all_to_all(local, "row", 0, 0, tiled=True)
    block = jnp.sum(pieces.reshape(4, STATE_ROWS // 4, 128), axis=0)
    along_z, total = ring_prefix(block, 1)
    along_x, total = ring_prefix(total, 4)
    along_y, _ = ring_prefix(total, 16)
    return lax.all_gather(block + along_z + along_x + along_y, "row", axis=0, tiled=True)


def line_weights(first_weight, second_weight):
    shard = jnp.concatenate([first_weight, second_weight.T], axis=0)
    line = lax.all_gather(shard, BOTH, axis=0, axis_index_groups=line_groups())
    line = line.reshape(4, 4, 55, 512)
    first = jnp.transpose(line[:, :, :35], (0, 2, 1, 3)).reshape(LINE_K, PROJ)
    first = jnp.pad(first, ((0, LINE_PAD - LINE_K), (0, 0)))
    second = jnp.transpose(line[:, :, 35:], (0, 2, 1, 3)).reshape(AHEAD_DIM, PROJ)
    return jnp.concatenate([first, second], axis=0)


def per_device(
    latent,
    query_raw,
    key_raw,
    value_raw,
    query_gain,
    key_gain,
    space_kernel,
    time_kernel,
    first_weight,
    first_bias,
    second_weight,
    second_bias,
    target_keys,
    target_values,
):
    line = line_weights(first_weight, second_weight)
    weights = lax.all_gather(line, BOTH, axis=0, axis_index_groups=plane_groups())
    key_raw, _ = lax.optimization_barrier((key_raw, line))

    across = [(i, i ^ 2) for i in range(4)]
    beside = [(i, i ^ 1) for i in range(4)]
    targets = []
    for mine in (target_keys, target_values):
        other = lax.ppermute(mine, "row", across)
        chip = jnp.concatenate([mine, other], axis=1)
        partner = lax.ppermute(chip, "row", beside)
        targets.append(jnp.concatenate([chip, partner], axis=1))

    local = local_state(
        key_raw.reshape(TOKENS, D), value_raw.reshape(TOKENS, D), key_gain.reshape(1, D)
    )
    state = state_prefix(local)
    hidden = apply_state(
        query_raw.reshape(TOKENS, D), latent.reshape(TOKENS, D), query_gain.reshape(1, D), state
    ).reshape(2, 2, 40, D)
    count = lax.axis_size("tm")
    forward = [(i, i + 1) for i in range(count - 1)]
    backward = [(i + 1, i) for i in range(count - 1)]
    before = lax.ppermute(hidden[1], "tm", forward)
    after = lax.ppermute(hidden[0], "tm", backward)
    down = [(i, i + 1) for i in range(3)]
    up = [(i + 1, i) for i in range(3)]
    above = lax.ppermute(hidden[:, 1], "row", down)
    below = lax.ppermute(hidden[:, 0], "row", up)
    blended, tokens = mix(
        hidden, before, after, above, below, space_kernel.reshape(9, D), time_kernel
    )
    attended = project_attend(
        tokens,
        first_bias.reshape(1, PROJ),
        second_bias.reshape(1, OUTF),
        targets[0],
        targets[1],
        weights,
    )
    return (blended, attended.reshape(2, 2, 40, OUTF))


def solution(mesh):
    return jax.shard_map(
        per_device,
        mesh=mesh,
        in_specs=(
            P("tm", "row", None, None),
            P("tm", "row", None, None),
            P("tm", "row", None, None),
            P("tm", "row", None, None),
            P(),
            P(),
            P(),
            P(),
            P("tm", "row"),
            P(),
            P("row", "tm"),
            P(),
            P("tm", "row", None),
            P("tm", "row", None),
        ),
        out_specs=(P("tm", "row", None, None), P("tm", "row", None, None)),
        check_vma=False,
    )
```

time: 1400 us -> 171 us (0.12)
  waiting for transfers between devices: 1130 us -> 32.8 us
  other arithmetic: 91.3 us -> 5.29 us
  local copies, waits for them, and re-layouts: 73.7 us -> 5.61 us
  Pallas kernels: 0 us -> 37.1 us
  matrix products: 29.4 us -> 0 us
  starting transfers between devices: 22.6 us -> 37.8 us
    unnamed x8 -> x1, waiting for transfers between devices: 641 us -> 0.02 us
    all_gather x5 -> x1, waiting for transfers between devices: 462 us -> 11.4 us  [per_device(): lax.all_gather(line, BOTH, axis=0, axis_index_groups=plane_groups())]
    select_n x128 -> x0, other arithmetic: 67.8 us -> none  [lap(): return jax.tree.map(lambda a, b: jnp.where(reached, a, b), new, before)]
    pallas_call x0 -> x4, Pallas kernels: none -> 37.1 us  [the longest x1 18.1 us: project_attend(): pl.pallas_call(project_kernel, in_specs=[vmem] * 5 + [pl.BlockSpec(memory...]
    dot_general x6 -> x0, matrix products: 29.4 us -> none  [the longest x1 8.85 us: per_device(): jnp.einsum('crwhd,dhe->crwhe', query_feat, key_state, precision=lax.Preci...]
    all_gather x2, blocking collectives: 13.9 us -> 37 us  [the longest x1 23.8 us: line_weights(): line = lax.all_gather(shard, BOTH, axis=0, axis_index_groups=line_groups())]
    unnamed x59 -> x21, local copies, waits for them, and re-layouts: 21.8 us -> 1.18 us
    reshape x9 -> x4, local copies, waits for them, and re-layouts: 21.4 us -> 2.51 us  [the longest x1 0.7 us: per_device(): space_kernel.reshape(9, D)]
  transfers between devices with their start and end apart: 11 -> 19, of which waited for: 10 -> 6; matrix products, arithmetic and copies ran while one was open for 4% -> 4% of each run, Pallas kernels for 0% -> 11%
where the time goes in v1:
time: 171 us; the launch traced here: 170 us
  starting transfers between devices  37.8 us (22%)
  Pallas kernels  37.1 us (22%)
  blocking collectives  37 us (22%)
  waiting for transfers between devices  32.8 us (19%)
  between operations  14.2 us (8%)
  local copies, waits for them, and re-layouts  5.61 us (3%)
  other arithmetic  5.29 us (3%)
    all_gather x1, blocking collectives, line_weights(): line = lax.all_gather(shard, BOTH, axis=0, axis_index_groups=line_groups())  23.8 us
    pallas_call x1, Pallas kernels, project_attend(): pl.pallas_call(project_kernel, in_specs=[vmem] * 5 + [pl.BlockSpec(memory...  18.1 us
    all_gather x1, blocking collectives, state_prefix(): lax.all_gather(block + along_z + along_x + along_y, 'row', axis=0, tiled=...  13.2 us
    ppermute x9, starting transfers between devices, shifted(): return lax.ppermute(value, 'tm', pairs)  12.1 us
    ppermute x1, waiting for transfers between devices, per_device(): after = lax.ppermute(hidden[0], 'tm', backward)  12.1 us
    all_gather x1, waiting for transfers between devices, per_device(): lax.all_gather(line, BOTH, axis=0, axis_index_groups=plane_groups())  11.4 us
    ppermute x2, starting transfers between devices, per_device(): partner = lax.ppermute(chip, 'row', beside)  10 us
    pallas_call x1, Pallas kernels, apply_state(): pl.pallas_call(apply_kernel, grid=(STEPS,), in_specs=[pl.BlockSpec((TOKEN...  7.43 us
  transfers between devices with their start and end apart: 19, of which 6 were waited for; matrix products, arithmetic and copies ran while one was open for 4% of the time, Pallas kernels for 11%

profile of v1, /device:TPU:1, one launch (start us, length us, event | category | flops | bytes accessed | tf_op | source)
XLA Modules:
  0.0 169.9 jit_solution(1949302306369705175)
XLA Ops:
  8.0 23.8 %all-gather.2 = bf16[16,55,512]{2,1,0:T(8,128)(2,1)S(1)} all-gather(bf16[1,55,512]{2,1,0:T(8,128)(2,1)S(1)} %maximum_bitcast_fusion), channel_id=2, replica_groups={{0,1,2,3,4,5,6,7,8,9,10,11,12,13,14,15},{16,17,18,19,20,21,22,23,24,25,..., dimensions={0}, use_global_device_ids=true | all-gather | bytes 957440 | tf_op jit(solution)/shard_map/all_gather | solution.py:330
  34.7 5.9 %local_state.1 = f32[608,128]{1,0:T(8,128)} custom-call(bf16[160,2240]{1,0:T(8,128)(2,1)} %bitcast.45, bf16[160,2240]{1,0:T(8,128)(2,1)} %bitcast.46, f32[1,2240]{1,0:T(1,128)} %reshape.62.gain_ref), custom_call_target="tpu_custom_call" | custom-call | tf_op jit(solution)/shard_map/local_state/pallas_call | solution.py:83
  40.5 3.6 %all-to-all-start = ((f32[4,152,128]{2,1,0:T(8,128)}), f32[4,152,128]{2,1,0:T(8,128)S(1)}, u32[]{:S(2)}, u32[]{:S(2)}) async-start(f32[4,152,128]{2,1,0:T(8,128)} %bitcast.44), calls=%async_computation | async-start | bytes 622592 | tf_op jit(solution)/shard_map/all_to_all | solution.py:320
  44.1 1.4 collective-permute-start.13
  45.5 4.3 %all-to-all-done = f32[4,152,128]{2,1,0:T(8,128)S(1)} async-done(((f32[4,152,128]{2,1,0:T(8,128)}), f32[4,152,128]{2,1,0:T(8,128)S(1)}, u32[]{:S(2)}, u32[]{:S(2)}) %all-to-all-start) | async-done | bytes 311328 | tf_op jit(solution)/shard_map/all_to_all | solution.py:320
  49.9 3.1 %collective-permute-start.1 = (f32[152,128]{1,0:T(8,128)S(1)}, f32[152,128]{1,0:T(8,128)S(1)}, u32[]{:S(2)}, u32[]{:S(2)}) collective-permute-start(f32[152,128]{1,0:T(8,128)S(1)} %reduce_sum.9), channel_id=1, source_target_pairs={{0,8},{4,12},{8,0},{12,4},{16,24},{20,28},{24,16},{28,20},{32,40},... | collective-permute-start | bytes 233480 | tf_op jit(solution)/shard_map/ppermute | solution.py:309
  53.0 1.2 collective-permute-start
  56.6 2.6 %collective-permute-done.1 = f32[152,128]{1,0:T(8,128)S(1)} collective-permute-done((f32[152,128]{1,0:T(8,128)S(1)}, f32[152,128]{1,0:T(8,128)S(1)}, u32[]{:S(2)}, u32[]{:S(2)}) %collective-permute-start.1) | collective-permute-done | bytes 77856 | tf_op jit(solution)/shard_map/ppermute | solution.py:309
  59.2 2.3 %collective-permute-done = f32[152,128]{1,0:T(8,128)S(1)} collective-permute-done((f32[152,128]{1,0:T(8,128)S(1)}, f32[152,128]{1,0:T(8,128)S(1)}, u32[]{:S(2)}, u32[]{:S(2)}) %collective-permute-start) | collective-permute-done | bytes 77856 | tf_op jit(solution)/shard_map/ppermute | solution.py:309
  61.5 2.8 %collective-permute-start.5 = (f32[152,128]{1,0:T(8,128)S(1)}, f32[152,128]{1,0:T(8,128)S(1)}, u32[]{:S(2)}, u32[]{:S(2)}) collective-permute-start(f32[152,128]{1,0:T(8,128)S(1)} %add_add_fusion.2), channel_id=1, source_target_pairs={{0,48},{4,52},{8,56},{12,60},{16,0},{20,4},{24,8},{28,12},{32,16},... | collective-permute-start | bytes 233480 | tf_op jit(solution)/shard_map/ppermute | solution.py:309
  65.5 4.3 %collective-permute-start.14 = (bf16[2,128,1280]{2,1,0:T(8,128)(2,1)S(1)}, bf16[2,128,1280]{2,1,0:T(8,128)(2,1)S(1)}, u32[]{:S(2)}, u32[]{:S(2)}) collective-permute-start(bf16[2,128,1280]{2,1,0:T(8,128)(2,1)S(1)} %pad_maximum_fusion.2), channel_id=1, source_target_pairs={{0,1},{1,0},{2,3},{3,2},{4,5},{5,4},{6,7},{7,6},{8,9},{9,8},{10,11... | collective-permute-start | bytes 1966088 | tf_op jit(solution)/shard_map/ppermute | solution.py:364
  69.9 2.8 %collective-permute-start.8 = (f32[152,128]{1,0:T(8,128)S(1)}, f32[152,128]{1,0:T(8,128)S(1)}, u32[]{:S(2)}, u32[]{:S(2)}) collective-permute-start(f32[152,128]{1,0:T(8,128)S(1)} %add_add_fusion.1), channel_id=1, source_target_pairs={{0,192},{4,196},{8,200},{12,204},{16,208},{20,212},{24,216},{28,22... | collective-permute-start | bytes 233480 | tf_op jit(solution)/shard_map/ppermute | solution.py:309
  74.7 5.7 %collective-permute-start.16 = (bf16[2,128,1280]{2,1,0:T(8,128)(2,1)}, bf16[2,128,1280]{2,1,0:T(8,128)(2,1)S(1)}, u32[]{:S(2)}, u32[]{:S(2)}) collective-permute-start(bf16[2,128,1280]{2,1,0:T(8,128)(2,1)} %pad_maximum_fusion.3), channel_id=1, source_target_pairs={{0,1},{1,0},{2,3},{3,2},{4,5},{5,4},{6,7},{7,6},{8,9},{9,8},{10,11... | collective-permute-start | bytes 1966088 | tf_op jit(solution)/shard_map/ppermute | solution.py:364
  80.4 13.2 %all_gather.17.state_ref = f32[608,128]{1,0:T(8,128)} all-gather(f32[152,128]{1,0:T(8,128)S(1)} %add_add_fusion), channel_id=1, replica_groups=mesh['tm'=64,'row'=4] {'row'}, dimensions={0}, use_global_device_ids=true | all-gather | bytes 389120 | tf_op jit(solution)/shard_map/all_gather | solution.py:325
  93.6 7.4 %apply_state.1 = bf16[160,2240]{1,0:T(8,128)(2,1)} custom-call(bf16[160,2240]{1,0:T(8,128)(2,1)} %bitcast.47, bf16[160,2240]{1,0:T(8,128)(2,1)} %bitcast.48, f32[1,2240]{1,0:T(1,128)} %reshape.56.gain_ref, f32[608,128]{1,0:T(8,128)} %all_gather.17.state_ref), custom_call_target="tpu_custom_call" | custom-call | tf_op jit(solution)/shard_map/apply_state/pallas_call | solution.py:121
  101.1 1.2 fusion.2
  102.3 3.7 %collective-permute-start.9 = (bf16[2,40,2240]{2,1,0:T(8,128)(2,1)S(1)}, bf16[2,40,2240]{2,1,0:T(8,128)(2,1)}, u32[]{:S(2)}, u32[]{:S(2)}) collective-permute-start(bf16[2,40,2240]{2,1,0:T(8,128)(2,1)S(1)} %bitcast.51), channel_id=1, source_target_pairs={{0,4},{4,8},{8,12},{12,16},{16,20},{20,24},{24,28},{28,32},{32,36}... | collective-permute-start | bytes 1075208 | tf_op jit(solution)/shard_map/ppermute | solution.py:377
  106.0 1.5 collective-permute-start.10
  107.6 2.6 %collective-permute-start.11 = (bf16[2,40,2240]{2,1,0:T(8,128)(2,1)S(1)}, bf16[2,40,2240]{2,1,0:T(8,128)(2,1)}, u32[]{:S(2)}, u32[]{:S(2)}) collective-permute-start(bf16[2,40,2240]{2,1,0:T(8,128)(2,1)S(1)} %get-tuple-element.9), channel_id=1, source_target_pairs={{0,1},{1,2},{2,3},{4,5},{5,6},{6,7},{8,9},{9,10},{10,11},{12,13},{... | collective-permute-start | bytes 1075208 | tf_op jit(solution)/shard_map/ppermute | solution.py:381
  110.2 2.5 %collective-permute-start.12 = (bf16[2,40,2240]{2,1,0:T(8,128)(2,1)S(1)}, bf16[2,40,2240]{2,1,0:T(8,128)(2,1)S(1)}, u32[]{:S(2)}, u32[]{:S(2)}) collective-permute-start(bf16[2,40,2240]{2,1,0:T(8,128)(2,1)S(1)} %get-tuple-element.8), channel_id=1, source_target_pairs={{1,0},{2,1},{3,2},{5,4},{6,5},{7,6},{9,8},{10,9},{11,10},{13,12},{... | collective-permute-start | bytes 1075208 | tf_op jit(solution)/shard_map/ppermute | solution.py:382
  115.0 12.1 %collective-permute-done.10.after_ref = bf16[2,40,2240]{2,1,0:T(8,128)(2,1)} collective-permute-done((bf16[2,40,2240]{2,1,0:T(8,128)(2,1)S(1)}, bf16[2,40,2240]{2,1,0:T(8,128)(2,1)}, u32[]{:S(2)}, u32[]{:S(2)}) %collective-permute-start.10) | collective-permute-done | bytes 358432 | tf_op jit(solution)/shard_map/ppermute | solution.py:378
  127.9 5.7 %mix.1 = (bf16[2,2,40,2240]{3,2,1,0:T(8,128)(2,1)}, bf16[160,2304]{1,0:T(8,128)(2,1)}) custom-call(bf16[2,2,40,2240]{3,2,1,0:T(8,128)(2,1)} %bitcast.35, bf16[2,40,2240]{2,1,0:T(8,128)(2,1)} %collective-permute-done.9.before_ref, bf16[2,40,2240]{2,1,0:T(8,128)(2,1)} %collective-permute-done.10.after_ref, ...), custom_call_target="tpu_custom_call" | custom-call | tf_op jit(solution)/shard_map/mix/pallas_call | solution.py:188
  133.6 11.4 %all-gather.5.cloned.1.call-done = bf16[3584,2048]{1,0:T(8,128)(2,1)} async-done(((bf16[224,2048]{1,0:T(8,128)(2,1)}), bf16[3584,2048]{1,0:T(8,128)(2,1)}) %all-gather.5.cloned.1.call-update) | async-done | bytes 14680080 | tf_op jit(solution)/shard_map/all_gather | solution.py:355
  145.0 18.1 %project_attend.1 = bf16[160,1280]{1,0:T(8,128)(2,1)} custom-call(bf16[160,2304]{1,0:T(8,128)(2,1)} %get-tuple-element.7.token_ref, f32[1,2048]{1,0:T(1,128)} %bitcast.53, f32[1,1280]{1,0:T(1,128)} %reshape.66.second_bias_ref, bf16[2,256,1280]{2,1,0:T(8,128)(2,1)} %pad_maximum_fusion.key_ref, bf16[2,256,1280]{2,1,0:T(8,128)(2,1)} %pad_maximum_fusion.1.value_ref, ...), custom_call_target="tpu_custom_call" | custom-call | tf_op jit(solution)/shard_map/project_attend/pallas_call | solution.py:279
  (62 shorter events, 12.5 us)
Async XLA Ops:
  7.2 137.8 %all-gather.5.cloned.1.call-start = ((), (), s32[]{:S(2)}) async-start(), calls=%async_computation.1 | async-start | bytes 15597568 | tf_op jit(solution)/shard_map/all_gather | solution.py:355
  34.0 10.1 %copy-start.1 = (bf16[2,64,1280]{2,1,0:T(8,128)(2,1)S(1)}, bf16[2,64,1280]{2,1,0:T(8,128)(2,1)}, u32[]{:S(2)}) copy-start(bf16[2,64,1280]{2,1,0:T(8,128)(2,1)} %param.26) | copy-start | bytes 983044
  34.0 20.2 %copy-start.2 = (bf16[2,64,1280]{2,1,0:T(8,128)(2,1)S(1)}, bf16[2,64,1280]{2,1,0:T(8,128)(2,1)}, u32[]{:S(2)}) copy-start(bf16[2,64,1280]{2,1,0:T(8,128)(2,1)} %param.27) | copy-start | bytes 983044
  34.0 20.7 %copy-start.7 = (f32[2240]{0:T(1024)S(1)}, f32[2240]{0:T(1024)}, u32[]{:S(2)}) copy-start(f32[2240]{0:T(1024)} %param.18) | copy-start | bytes 26884
  34.0 21.3 %copy-start.5 = (f32[3,3,2240]{2,1,0:T(4,128)S(1)}, f32[3,3,2240]{2,1,0:T(4,128)}, u32[]{:S(2)}) copy-start(f32[3,3,2240]{2,1,0:T(4,128)} %param.20) | copy-start | bytes 241924
  34.1 22.0 %copy-start.8 = (f32[1280]{0:T(1024)S(1)}, f32[1280]{0:T(1024)}, u32[]{:S(2)}) copy-start(f32[1280]{0:T(1024)} %param.25) | copy-start | bytes 15364
  40.5 9.3 %all-to-all-start = ((f32[4,152,128]{2,1,0:T(8,128)}), f32[4,152,128]{2,1,0:T(8,128)S(1)}, u32[]{:S(2)}, u32[]{:S(2)}) async-start(f32[4,152,128]{2,1,0:T(8,128)} %bitcast.44), calls=%async_computation | async-start | bytes 622592 | tf_op jit(solution)/shard_map/all_to_all | solution.py:320
  44.1 21.3 %collective-permute-start.13 = (bf16[2,64,1280]{2,1,0:T(8,128)(2,1)S(1)}, bf16[2,64,1280]{2,1,0:T(8,128)(2,1)S(1)}, u32[]{:S(2)}, u32[]{:S(2)}) collective-permute-start(bf16[2,64,1280]{2,1,0:T(8,128)(2,1)S(1)} %copy-done.1), channel_id=1, source_target_pairs={{0,2},{1,3},{2,0},{3,1},{4,6},{5,7},{6,4},{7,5},{8,10},{9,11},{10,... | collective-permute-start | bytes 983048 | tf_op jit(solution)/shard_map/ppermute | solution.py:362
  49.8 6.8 %collective-permute-start.2 = (f32[152,128]{1,0:T(8,128)S(1)}, f32[152,128]{1,0:T(8,128)S(1)}, u32[]{:S(2)}, u32[]{:S(2)}) collective-permute-start(f32[152,128]{1,0:T(8,128)S(1)} %reduce_sum.9), channel_id=1, source_target_pairs={{0,12},{4,0},{8,4},{12,8},{16,28},{20,16},{24,20},{28,24},{32,44},... | collective-permute-start | bytes 233480 | tf_op jit(solution)/shard_map/ppermute | solution.py:309
  49.9 9.3 %collective-permute-start.1 = (f32[152,128]{1,0:T(8,128)S(1)}, f32[152,128]{1,0:T(8,128)S(1)}, u32[]{:S(2)}, u32[]{:S(2)}) collective-permute-start(f32[152,128]{1,0:T(8,128)S(1)} %reduce_sum.9), channel_id=1, source_target_pairs={{0,8},{4,12},{8,0},{12,4},{16,24},{20,28},{24,16},{28,20},{32,40},... | collective-permute-start | bytes 233480 | tf_op jit(solution)/shard_map/ppermute | solution.py:309
  53.0 8.5 %collective-permute-start = (f32[152,128]{1,0:T(8,128)S(1)}, f32[152,128]{1,0:T(8,128)S(1)}, u32[]{:S(2)}, u32[]{:S(2)}) collective-permute-start(f32[152,128]{1,0:T(8,128)S(1)} %reduce_sum.9), channel_id=1, source_target_pairs={{0,4},{4,8},{8,12},{12,0},{16,20},{20,24},{24,28},{28,16},{32,36},... | collective-permute-start | bytes 233480 | tf_op jit(solution)/shard_map/ppermute | solution.py:309
  54.2 19.6 %collective-permute-start.15 = (bf16[2,64,1280]{2,1,0:T(8,128)(2,1)S(1)}, bf16[2,64,1280]{2,1,0:T(8,128)(2,1)S(1)}, u32[]{:S(2)}, u32[]{:S(2)}) collective-permute-start(bf16[2,64,1280]{2,1,0:T(8,128)(2,1)S(1)} %copy-done.2), channel_id=1, source_target_pairs={{0,2},{1,3},{2,0},{3,1},{4,6},{5,7},{6,4},{7,5},{8,10},{9,11},{10,... | collective-permute-start | bytes 983048 | tf_op jit(solution)/shard_map/ppermute | solution.py:362
  61.5 8.3 %collective-permute-start.5 = (f32[152,128]{1,0:T(8,128)S(1)}, f32[152,128]{1,0:T(8,128)S(1)}, u32[]{:S(2)}, u32[]{:S(2)}) collective-permute-start(f32[152,128]{1,0:T(8,128)S(1)} %add_add_fusion.2), channel_id=1, source_target_pairs={{0,48},{4,52},{8,56},{12,60},{16,0},{20,4},{24,8},{28,12},{32,16},... | collective-permute-start | bytes 233480 | tf_op jit(solution)/shard_map/ppermute | solution.py:309
  64.3 5.5 %collective-permute-start.4 = (f32[152,128]{1,0:T(8,128)S(1)}, f32[152,128]{1,0:T(8,128)S(1)}, u32[]{:S(2)}, u32[]{:S(2)}) collective-permute-start(f32[152,128]{1,0:T(8,128)S(1)} %add_add_fusion.2), channel_id=1, source_target_pairs={{0,32},{4,36},{8,40},{12,44},{16,48},{20,52},{24,56},{28,60},{32,0... | collective-permute-start | bytes 233480 | tf_op jit(solution)/shard_map/ppermute | solution.py:309
  64.8 5.1 %collective-permute-start.3 = (f32[152,128]{1,0:T(8,128)S(1)}, f32[152,128]{1,0:T(8,128)S(1)}, u32[]{:S(2)}, u32[]{:S(2)}) collective-permute-start(f32[152,128]{1,0:T(8,128)S(1)} %add_add_fusion.2), channel_id=1, source_target_pairs={{0,16},{4,20},{8,24},{12,28},{16,32},{20,36},{24,40},{28,44},{32,4... | collective-permute-start | bytes 233480 | tf_op jit(solution)/shard_map/ppermute | solution.py:309
  65.5 44.7 %collective-permute-start.14 = (bf16[2,128,1280]{2,1,0:T(8,128)(2,1)S(1)}, bf16[2,128,1280]{2,1,0:T(8,128)(2,1)S(1)}, u32[]{:S(2)}, u32[]{:S(2)}) collective-permute-start(bf16[2,128,1280]{2,1,0:T(8,128)(2,1)S(1)} %pad_maximum_fusion.2), channel_id=1, source_target_pairs={{0,1},{1,0},{2,3},{3,2},{4,5},{5,4},{6,7},{7,6},{8,9},{9,8},{10,11... | collective-permute-start | bytes 1966088 | tf_op jit(solution)/shard_map/ppermute | solution.py:364
  69.9 10.4 %collective-permute-start.8 = (f32[152,128]{1,0:T(8,128)S(1)}, f32[152,128]{1,0:T(8,128)S(1)}, u32[]{:S(2)}, u32[]{:S(2)}) collective-permute-start(f32[152,128]{1,0:T(8,128)S(1)} %add_add_fusion.1), channel_id=1, source_target_pairs={{0,192},{4,196},{8,200},{12,204},{16,208},{20,212},{24,216},{28,22... | collective-permute-start | bytes 233480 | tf_op jit(solution)/shard_map/ppermute | solution.py:309
  72.7 7.6 %collective-permute-start.7 = (f32[152,128]{1,0:T(8,128)S(1)}, f32[152,128]{1,0:T(8,128)S(1)}, u32[]{:S(2)}, u32[]{:S(2)}) collective-permute-start(f32[152,128]{1,0:T(8,128)S(1)} %add_add_fusion.1), channel_id=1, source_target_pairs={{0,128},{4,132},{8,136},{12,140},{16,144},{20,148},{24,152},{28,15... | collective-permute-start | bytes 233480 | tf_op jit(solution)/shard_map/ppermute | solution.py:309
  73.1 7.3 %collective-permute-start.6 = (f32[152,128]{1,0:T(8,128)S(1)}, f32[152,128]{1,0:T(8,128)S(1)}, u32[]{:S(2)}, u32[]{:S(2)}) collective-permute-start(f32[152,128]{1,0:T(8,128)S(1)} %add_add_fusion.1), channel_id=1, source_target_pairs={{0,64},{4,68},{8,72},{12,76},{16,80},{20,84},{24,88},{28,92},{32,9... | collective-permute-start | bytes 233480 | tf_op jit(solution)/shard_map/ppermute | solution.py:309
  74.7 39.2 %collective-permute-start.16 = (bf16[2,128,1280]{2,1,0:T(8,128)(2,1)}, bf16[2,128,1280]{2,1,0:T(8,128)(2,1)S(1)}, u32[]{:S(2)}, u32[]{:S(2)}) collective-permute-start(bf16[2,128,1280]{2,1,0:T(8,128)(2,1)} %pad_maximum_fusion.3), channel_id=1, source_target_pairs={{0,1},{1,0},{2,3},{3,2},{4,5},{5,4},{6,7},{7,6},{8,9},{9,8},{10,11... | collective-permute-start | bytes 1966088 | tf_op jit(solution)/shard_map/ppermute | solution.py:364
  102.3 12.7 %collective-permute-start.9 = (bf16[2,40,2240]{2,1,0:T(8,128)(2,1)S(1)}, bf16[2,40,2240]{2,1,0:T(8,128)(2,1)}, u32[]{:S(2)}, u32[]{:S(2)}) collective-permute-start(bf16[2,40,2240]{2,1,0:T(8,128)(2,1)S(1)} %bitcast.51), channel_id=1, source_target_pairs={{0,4},{4,8},{8,12},{12,16},{16,20},{20,24},{24,28},{28,32},{32,36}... | collective-permute-start | bytes 1075208 | tf_op jit(solution)/shard_map/ppermute | solution.py:377
  106.0 21.1 %collective-permute-start.10 = (bf16[2,40,2240]{2,1,0:T(8,128)(2,1)S(1)}, bf16[2,40,2240]{2,1,0:T(8,128)(2,1)}, u32[]{:S(2)}, u32[]{:S(2)}) collective-permute-start(bf16[2,40,2240]{2,1,0:T(8,128)(2,1)S(1)} %bitcast.50), channel_id=1, source_target_pairs={{4,0},{8,4},{12,8},{16,12},{20,16},{24,20},{28,24},{32,28},{36,32}... | collective-permute-start | bytes 1075208 | tf_op jit(solution)/shard_map/ppermute | solution.py:378
  107.6 19.6 %collective-permute-start.11 = (bf16[2,40,2240]{2,1,0:T(8,128)(2,1)S(1)}, bf16[2,40,2240]{2,1,0:T(8,128)(2,1)}, u32[]{:S(2)}, u32[]{:S(2)}) collective-permute-start(bf16[2,40,2240]{2,1,0:T(8,128)(2,1)S(1)} %get-tuple-element.9), channel_id=1, source_target_pairs={{0,1},{1,2},{2,3},{4,5},{5,6},{6,7},{8,9},{9,10},{10,11},{12,13},{... | collective-permute-start | bytes 1075208 | tf_op jit(solution)/shard_map/ppermute | solution.py:381
  110.2 17.0 %collective-permute-start.12 = (bf16[2,40,2240]{2,1,0:T(8,128)(2,1)S(1)}, bf16[2,40,2240]{2,1,0:T(8,128)(2,1)S(1)}, u32[]{:S(2)}, u32[]{:S(2)}) collective-permute-start(bf16[2,40,2240]{2,1,0:T(8,128)(2,1)S(1)} %get-tuple-element.8), channel_id=1, source_target_pairs={{1,0},{2,1},{3,2},{5,4},{6,5},{7,6},{9,8},{10,9},{11,10},{13,12},{... | collective-permute-start | bytes 1075208 | tf_op jit(solution)/shard_map/ppermute | solution.py:382
  (4 other events, 12.3 us)
Sparse Core Ops, SparseCore 0:
  34.2 110.7 all-gather.4
